TPU v7x, 512 devices: a whole 4x4x16 slice. The times are simulated.
512 devices in a mesh: segment: 2 (over x_lo), seq: 32 (over z, core), tensor: 8 (over y, x_hi).
Axes of the slice: x: 4 (x_hi: 2, x_lo: 2; x = x_hi * 2 + x_lo), y: 4, z: 16, core: 2. Of those that a mesh axis runs over, the one named last changes fastest.
Arguments:
- vision_states: bfloat16 [6144, 7680], P(('segment', 'seq'), 'tensor'), may hold values from -6 to 6
- kv_weight: bfloat16 [7680, 2048], P('tensor'), may hold values from -0.09375 to 0.09375
- key_gain: float32 [128], replicated, may hold values from 0.5 to 1.5
- queries: bfloat16 [16384, 8, 1024], P('seq', 'tensor', 'segment'), may hold values from -700 to 700
- tile_tokens: int32 [4], replicated, may hold values from 768 to 1536, as said below
- text_tiles: int32 [16384, 2], P('seq'), may hold values from 0 to 4, as said below
Outputs:
- attended: bfloat16 [16384, 8, 1024], P('seq', 'tensor', 'segment')
Inputs may be any that keep to these rules, and one draw needn't show every extreme that they name: The valid tokens of tile i are its first tile_tokens[i] positions of 1536; some tile is full. Text token r sees tiles text_tiles[r, 0] to text_tiles[r, 1] - 1, with text_tiles[r, 0] <= text_tiles[r, 1]; an empty range means it sees no image.
All inputs are finite; a program needn't handle non-finite values.
Results may differ from a plain program's by a relative error of at most 0.012.
The roundings to bfloat16 on the way count: a program that leaves them out, or rounds other values in their place, can miss the bound.
Values may be sent and summed in bfloat16 or wider, within the bound.
A program may use at most 64 MiB of HBM per device.

v0:
```python
import jax
import jax.numpy as jnp
from jax import lax
from jax.sharding import PartitionSpec as P


def block_count(total_rows, limit_rows):
    for parts_count in range(1, total_rows + 1):
        if total_rows % parts_count == 0 and total_rows // parts_count <= limit_rows:
            return parts_count
    return total_rows


def visibility(positions, tile_len, tile_tokens, lower, upper):
    tile_ids = positions // tile_len
    within_tile = positions % tile_len
    tile_table = jnp.arange(tile_tokens.shape[0], dtype=jnp.int32)
    valid_count = jnp.sum(
        jnp.where(tile_ids[:, None] == tile_table[None, :], tile_tokens[None, :], 0), axis=-1
    )
    key_valid = within_tile < valid_count
    return (
        key_valid[None, :]
        & (tile_ids[None, :] >= lower[:, None])
        & (tile_ids[None, :] < upper[:, None])
    )


def update(running, query_heads, kv_piece, visible, score_scale, head_dim):
    row_max, row_sum, summed = running
    scores = (
        jnp.einsum(
            "rkhd,knd->rkhn",
            query_heads,
            kv_piece[:, :, :head_dim],
            preferred_element_type=jnp.float32,
        )
        * score_scale
    )
    key_mask = visible[:, None, None, :]
    masked = jnp.where(key_mask, scores, -1e30)
    new_max = jnp.maximum(row_max, jnp.max(masked, axis=-1))
    factor = jnp.exp(row_max - new_max)
    expterm = jnp.where(key_mask, jnp.exp(masked - new_max[..., None]), 0.0)
    row_sum = row_sum * factor + jnp.sum(expterm, axis=-1)
    weights = expterm.astype(jnp.bfloat16)
    summed = summed * factor[..., None] + jnp.einsum(
        "rkhn,knd->rkhd", weights, kv_piece[:, :, head_dim:], preferred_element_type=jnp.float32
    )
    return (new_max, row_sum, summed)


def shards(vision_states, kv_weight, key_gain, queries, tile_tokens, text_tiles):
    head_dim = key_gain.shape[0]
    key_rows = vision_states.shape[0]
    all_heads = kv_weight.shape[1] // (2 * head_dim)
    local_heads = all_heads // lax.axis_size("tensor")
    weight_heads = kv_weight.reshape(kv_weight.shape[0], all_heads, 2 * head_dim)
    sums = lax.psum_scatter(
        jnp.einsum("rd,dch->crh", vision_states, weight_heads, preferred_element_type=jnp.float32),
        "tensor",
        scatter_dimension=0,
        tiled=True,
    )
    keys_raw = sums[:, :, :head_dim]
    mean_sq = jnp.mean(keys_raw * keys_raw, axis=-1, keepdims=True)
    normed = keys_raw * lax.rsqrt(mean_sq + 1e-05) * key_gain
    kv_block = jnp.concatenate([normed, sums[:, :, head_dim:]], axis=-1).astype(jnp.bfloat16)
    segment_count = lax.axis_size("segment")
    seq_count = lax.axis_size("seq")
    tile_len = key_rows * segment_count * seq_count // tile_tokens.shape[0]
    text_rows = queries.shape[0]
    query_count = queries.shape[2] // head_dim
    query_heads = queries.reshape(text_rows, local_heads, query_count, head_dim)
    lower = text_tiles[:, 0]
    upper = text_tiles[:, 1]
    unseen = (upper <= lower).astype(jnp.float32)
    score_scale = head_dim ** (-0.5)
    start_state = (
        jnp.full((text_rows, local_heads, query_count), -1e30, jnp.float32),
        jnp.zeros((text_rows, local_heads, query_count), jnp.float32),
        jnp.zeros((text_rows, local_heads, query_count, head_dim), jnp.float32),
    )
    gathered = lax.all_gather(kv_block, ("segment", "seq"), axis=1, tiled=True)
    total_rows = gathered.shape[1]
    blocks = block_count(total_rows, 768)
    block_rows = total_rows // blocks

    def one_block(block_index, state_now):
        block_piece = lax.dynamic_slice_in_dim(gathered, block_index * block_rows, block_rows, 1)
        local_rows = block_index * block_rows + jnp.arange(block_rows, dtype=jnp.int32)
        visible = visibility(local_rows, tile_len, tile_tokens, lower, upper)
        return update(state_now, query_heads, block_piece, visible, score_scale, head_dim)

    row_max, row_sum, summed = lax.fori_loop(0, blocks, one_block, start_state)
    attended = summed / (row_sum + unseen[:, None, None])[..., None]
    return attended.reshape(text_rows, local_heads, query_count * head_dim).astype(jnp.bfloat16)


def solution(mesh):
    placed = (
        P(("segment", "seq"), "tensor"),
        P("tensor", None),
        P(),
        P("seq", "tensor", "segment"),
        P(),
        P("seq", None),
    )
    return jax.shard_map(
        shards, mesh=mesh, in_specs=placed, out_specs=P("seq", "tensor", "segment"), check_vma=False
    )
```

profile of v0, /device:TPU:1, one launch (start us, length us, event | category | flops | bytes accessed | tf_op | source)
XLA Modules:
  0.0 335.9 jit_solution(15315524799468415300)
XLA Ops:
  6.5 0.0 copy-start
  6.5 0.0 reduce-scatter.2.cloned.1.call-start
  6.6 0.9 copy-done
  7.5 3.8 %fusion.30 = f32[8,96,256]{2,1,0:T(8,128)} fusion(bf16[120,8,8,256]{3,2,1,0:T(8,128)(2,1)} %bitcast.107, bf16[96,960]{1,0:T(8,128)(2,1)S(1)} %copy-done), kind=kOutput, calls=%fused_computation.41 | convolution fusion | flops 377487360 | bytes 4902912 | tf_op jit(solution)/shard_map/rd,dch->crh/dot_general | solution.py:60
  11.2 0.0 reduce-scatter.2.cloned.1.call-update
  11.2 0.0 all-gather.2.cloned.1.call-start
  11.3 90.3 %reduce-scatter.2.cloned.1.call-done = f32[1,96,256]{2,1,0:T(8,128)} async-done(((f32[8,96,256]{2,1,0:T(8,128)}), f32[1,96,256]{2,1,0:T(8,128)}) %reduce-scatter.2.cloned.1.call-update) | async-done | bytes 98320 | tf_op jit(solution)/shard_map/reduce_scatter | solution.py:59
  101.6 0.9 multiply_reduce_fusion
  102.5 0.8 slice.46
  103.3 0.9 multiply_convert_fusion
  104.2 0.6 pad_maximum_fusion
  104.8 0.0 all-gather.2.cloned.1.call-update
  104.9 0.0 copy-done.2
  104.9 0.2 copy.20
  105.1 0.3 copy.21
  105.4 0.0 copy-done.3
  105.5 124.5 %all-gather.2.cloned.1.call-done = bf16[1,6144,256]{2,1,0:T(8,128)(2,1)} async-done(((bf16[1,96,256]{2,1,0:T(8,128)(2,1)}), bf16[1,6144,256]{2,1,0:T(8,128)(2,1)}) %all-gather.2.cloned.1.call-update) | async-done | bytes 3145744 | tf_op jit(solution)/shard_map/all_gather | solution.py:84
  229.9 98.0 %while.20 = (s32[]{:T(128)}, f32[512,1,4]{0,2,1:T(4,128)S(1)}, f32[512,1,4]{0,2,1:T(4,128)S(1)}, f32[512,1,4,128]{0,3,2,1:T(8,128)S(1)}, s32[4]{0:T(128)S(1)}, /...) while((s32[]{:T(128)}, f32[512,1,4]{0,2,1:T(4,128)S(1)}, ...), condition=%wide.region_6.7_spmd.clone, body=%wide.region_2.6_spmd.clone.sunk | while | flops 828146688 | bytes 48780040 | solution.py:95
  229.9 0.1 select_reduce_fusion.2
  230.1 0.5 compare_and_fusion.2
  230.5 4.8 %fusion.43 = (f32[512,4]{0,1:T(4,128)S(1)}, f32[768,512,4]{1,0,2:T(8,128)}) fusion(pred[512,768]{0,1:T(8,128)(4,1)S(1)} %compare_and_fusion.2, bf16[512,1,4,128]{3,0,2,1:T(8,128)(2,1)S(1)} %get-tuple-element.402, bf16[1,6144,256]{2,1,0:T(8,128)(2,1)} %get-tuple-element.401, s32[]{:T(128)S(6)} %select_n.147), kind=kOutput, calls=%fused_computation.2.clone.1 | convolution fusion | flops 407369728 | bytes 7413764 | tf_op jit(solution)/shard_map/while/body/eval_jaxpr/rkhd,knd->rkhn/dot_general | solution.py:32
  235.4 5.2 %fusion.46 = f32[512,1,4,128]{0,3,2,1:T(8,128)S(1)} fusion(f32[768,512,4]{1,0,2:T(8,128)} %get-tuple-element.364, f32[512,4]{0,1:T(4,128)S(1)} %bitcast.100, pred[512,768]{0,1:T(8,128)(4,1)S(1)} %compare_and_fusion.2, f32[512,1,4,128]{0,3,2,1:T(8,128)S(1)} %get-tuple-element.383, f32[512,4]{0,1:T(4,128)S(1)} %get-tuple-element.365, ...), kind=kOutput, calls=%fused_computation.10.clone.1 | convolution fusion | flops 411303936 | bytes 8994825 | tf_op jit(solution)/shard_map/while/body/eval_jaxpr/rkhn,knd->rkhd/dot_general | solution.py:47
  240.5 0.0 copy-done.1
  240.6 1.6 fusion.45
  242.2 0.1 select_reduce_fusion.2
  242.3 0.5 compare_and_fusion.2
  242.8 4.8 %fusion.43 = (f32[512,4]{0,1:T(4,128)S(1)}, f32[768,512,4]{1,0,2:T(8,128)}) fusion(pred[512,768]{0,1:T(8,128)(4,1)S(1)} %compare_and_fusion.2, bf16[512,1,4,128]{3,0,2,1:T(8,128)(2,1)S(1)} %get-tuple-element.402, bf16[1,6144,256]{2,1,0:T(8,128)(2,1)} %get-tuple-element.401, s32[]{:T(128)S(6)} %select_n.147), kind=kOutput, calls=%fused_computation.2.clone.1 | convolution fusion | flops 407369728 | bytes 7413764 | tf_op jit(solution)/shard_map/while/body/eval_jaxpr/rkhd,knd->rkhn/dot_general | solution.py:32
  247.6 5.2 %fusion.46 = f32[512,1,4,128]{0,3,2,1:T(8,128)S(1)} fusion(f32[768,512,4]{1,0,2:T(8,128)} %get-tuple-element.364, f32[512,4]{0,1:T(4,128)S(1)} %bitcast.100, pred[512,768]{0,1:T(8,128)(4,1)S(1)} %compare_and_fusion.2, f32[512,1,4,128]{0,3,2,1:T(8,128)S(1)} %get-tuple-element.383, f32[512,4]{0,1:T(4,128)S(1)} %get-tuple-element.365, ...), kind=kOutput, calls=%fused_computation.10.clone.1 | convolution fusion | flops 411303936 | bytes 8994825 | tf_op jit(solution)/shard_map/while/body/eval_jaxpr/rkhn,knd->rkhd/dot_general | solution.py:47
  252.8 1.6 fusion.45
  254.5 0.1 select_reduce_fusion.2
  254.6 0.5 compare_and_fusion.2
  255.1 4.8 %fusion.43 = (f32[512,4]{0,1:T(4,128)S(1)}, f32[768,512,4]{1,0,2:T(8,128)}) fusion(pred[512,768]{0,1:T(8,128)(4,1)S(1)} %compare_and_fusion.2, bf16[512,1,4,128]{3,0,2,1:T(8,128)(2,1)S(1)} %get-tuple-element.402, bf16[1,6144,256]{2,1,0:T(8,128)(2,1)} %get-tuple-element.401, s32[]{:T(128)S(6)} %select_n.147), kind=kOutput, calls=%fused_computation.2.clone.1 | convolution fusion | flops 407369728 | bytes 7413764 | tf_op jit(solution)/shard_map/while/body/eval_jaxpr/rkhd,knd->rkhn/dot_general | solution.py:32
  259.9 5.2 %fusion.46 = f32[512,1,4,128]{0,3,2,1:T(8,128)S(1)} fusion(f32[768,512,4]{1,0,2:T(8,128)} %get-tuple-element.364, f32[512,4]{0,1:T(4,128)S(1)} %bitcast.100, pred[512,768]{0,1:T(8,128)(4,1)S(1)} %compare_and_fusion.2, f32[512,1,4,128]{0,3,2,1:T(8,128)S(1)} %get-tuple-element.383, f32[512,4]{0,1:T(4,128)S(1)} %get-tuple-element.365, ...), kind=kOutput, calls=%fused_computation.10.clone.1 | convolution fusion | flops 411303936 | bytes 8994825 | tf_op jit(solution)/shard_map/while/body/eval_jaxpr/rkhn,knd->rkhd/dot_general | solution.py:47
  265.1 1.6 fusion.45
  266.7 0.1 select_reduce_fusion.2
  266.8 0.5 compare_and_fusion.2
  267.3 4.8 %fusion.43 = (f32[512,4]{0,1:T(4,128)S(1)}, f32[768,512,4]{1,0,2:T(8,128)}) fusion(pred[512,768]{0,1:T(8,128)(4,1)S(1)} %compare_and_fusion.2, bf16[512,1,4,128]{3,0,2,1:T(8,128)(2,1)S(1)} %get-tuple-element.402, bf16[1,6144,256]{2,1,0:T(8,128)(2,1)} %get-tuple-element.401, s32[]{:T(128)S(6)} %select_n.147), kind=kOutput, calls=%fused_computation.2.clone.1 | convolution fusion | flops 407369728 | bytes 7413764 | tf_op jit(solution)/shard_map/while/body/eval_jaxpr/rkhd,knd->rkhn/dot_general | solution.py:32
  272.1 0.0 copy-start.1
  272.1 5.2 %fusion.46 = f32[512,1,4,128]{0,3,2,1:T(8,128)S(1)} fusion(f32[768,512,4]{1,0,2:T(8,128)} %get-tuple-element.364, f32[512,4]{0,1:T(4,128)S(1)} %bitcast.100, pred[512,768]{0,1:T(8,128)(4,1)S(1)} %compare_and_fusion.2, f32[512,1,4,128]{0,3,2,1:T(8,128)S(1)} %get-tuple-element.383, f32[512,4]{0,1:T(4,128)S(1)} %get-tuple-element.365, ...), kind=kOutput, calls=%fused_computation.10.clone.1 | convolution fusion | flops 411303936 | bytes 8994825 | tf_op jit(solution)/shard_map/while/body/eval_jaxpr/rkhn,knd->rkhd/dot_general | solution.py:47
  277.3 1.6 fusion.45
  279.0 0.1 select_reduce_fusion.2
  279.1 0.5 compare_and_fusion.2
  279.6 4.8 %fusion.43 = (f32[512,4]{0,1:T(4,128)S(1)}, f32[768,512,4]{1,0,2:T(8,128)}) fusion(pred[512,768]{0,1:T(8,128)(4,1)S(1)} %compare_and_fusion.2, bf16[512,1,4,128]{3,0,2,1:T(8,128)(2,1)S(1)} %get-tuple-element.402, bf16[1,6144,256]{2,1,0:T(8,128)(2,1)} %get-tuple-element.401, s32[]{:T(128)S(6)} %select_n.147), kind=kOutput, calls=%fused_computation.2.clone.1 | convolution fusion | flops 407369728 | bytes 7413764 | tf_op jit(solution)/shard_map/while/body/eval_jaxpr/rkhd,knd->rkhn/dot_general | solution.py:32
  284.4 5.2 %fusion.46 = f32[512,1,4,128]{0,3,2,1:T(8,128)S(1)} fusion(f32[768,512,4]{1,0,2:T(8,128)} %get-tuple-element.364, f32[512,4]{0,1:T(4,128)S(1)} %bitcast.100, pred[512,768]{0,1:T(8,128)(4,1)S(1)} %compare_and_fusion.2, f32[512,1,4,128]{0,3,2,1:T(8,128)S(1)} %get-tuple-element.383, f32[512,4]{0,1:T(4,128)S(1)} %get-tuple-element.365, ...), kind=kOutput, calls=%fused_computation.10.clone.1 | convolution fusion | flops 411303936 | bytes 8994825 | tf_op jit(solution)/shard_map/while/body/eval_jaxpr/rkhn,knd->rkhd/dot_general | solution.py:47
  289.6 0.0 copy-done.1
  289.6 1.6 fusion.45
  291.2 0.1 select_reduce_fusion.2
  291.3 0.5 compare_and_fusion.2
  291.8 4.8 %fusion.43 = (f32[512,4]{0,1:T(4,128)S(1)}, f32[768,512,4]{1,0,2:T(8,128)}) fusion(pred[512,768]{0,1:T(8,128)(4,1)S(1)} %compare_and_fusion.2, bf16[512,1,4,128]{3,0,2,1:T(8,128)(2,1)S(1)} %get-tuple-element.402, bf16[1,6144,256]{2,1,0:T(8,128)(2,1)} %get-tuple-element.401, s32[]{:T(128)S(6)} %select_n.147), kind=kOutput, calls=%fused_computation.2.clone.1 | convolution fusion | flops 407369728 | bytes 7413764 | tf_op jit(solution)/shard_map/while/body/eval_jaxpr/rkhd,knd->rkhn/dot_general | solution.py:32
  296.6 5.2 %fusion.46 = f32[512,1,4,128]{0,3,2,1:T(8,128)S(1)} fusion(f32[768,512,4]{1,0,2:T(8,128)} %get-tuple-element.364, f32[512,4]{0,1:T(4,128)S(1)} %bitcast.100, pred[512,768]{0,1:T(8,128)(4,1)S(1)} %compare_and_fusion.2, f32[512,1,4,128]{0,3,2,1:T(8,128)S(1)} %get-tuple-element.383, f32[512,4]{0,1:T(4,128)S(1)} %get-tuple-element.365, ...), kind=kOutput, calls=%fused_computation.10.clone.1 | convolution fusion | flops 411303936 | bytes 8994825 | tf_op jit(solution)/shard_map/while/body/eval_jaxpr/rkhn,knd->rkhd/dot_general | solution.py:47
  301.8 1.6 fusion.45
  303.5 0.1 select_reduce_fusion.2
  303.6 0.5 compare_and_fusion.2
  304.1 4.8 %fusion.43 = (f32[512,4]{0,1:T(4,128)S(1)}, f32[768,512,4]{1,0,2:T(8,128)}) fusion(pred[512,768]{0,1:T(8,128)(4,1)S(1)} %compare_and_fusion.2, bf16[512,1,4,128]{3,0,2,1:T(8,128)(2,1)S(1)} %get-tuple-element.402, bf16[1,6144,256]{2,1,0:T(8,128)(2,1)} %get-tuple-element.401, s32[]{:T(128)S(6)} %select_n.147), kind=kOutput, calls=%fused_computation.2.clone.1 | convolution fusion | flops 407369728 | bytes 7413764 | tf_op jit(solution)/shard_map/while/body/eval_jaxpr/rkhd,knd->rkhn/dot_general | solution.py:32
  308.9 5.2 %fusion.46 = f32[512,1,4,128]{0,3,2,1:T(8,128)S(1)} fusion(f32[768,512,4]{1,0,2:T(8,128)} %get-tuple-element.364, f32[512,4]{0,1:T(4,128)S(1)} %bitcast.100, pred[512,768]{0,1:T(8,128)(4,1)S(1)} %compare_and_fusion.2, f32[512,1,4,128]{0,3,2,1:T(8,128)S(1)} %get-tuple-element.383, f32[512,4]{0,1:T(4,128)S(1)} %get-tuple-element.365, ...), kind=kOutput, calls=%fused_computation.10.clone.1 | convolution fusion | flops 411303936 | bytes 8994825 | tf_op jit(solution)/shard_map/while/body/eval_jaxpr/rkhn,knd->rkhd/dot_general | solution.py:47
  314.1 0.0 copy-done.1
  314.1 1.6 fusion.45
  315.7 0.1 select_reduce_fusion.2
  315.8 0.5 compare_and_fusion.2
  316.3 4.8 %fusion.43 = (f32[512,4]{0,1:T(4,128)S(1)}, f32[768,512,4]{1,0,2:T(8,128)}) fusion(pred[512,768]{0,1:T(8,128)(4,1)S(1)} %compare_and_fusion.2, bf16[512,1,4,128]{3,0,2,1:T(8,128)(2,1)S(1)} %get-tuple-element.402, bf16[1,6144,256]{2,1,0:T(8,128)(2,1)} %get-tuple-element.401, s32[]{:T(128)S(6)} %select_n.147), kind=kOutput, calls=%fused_computation.2.clone.1 | convolution fusion | flops 407369728 | bytes 7413764 | tf_op jit(solution)/shard_map/while/body/eval_jaxpr/rkhd,knd->rkhn/dot_general | solution.py:32
  321.1 5.2 %fusion.46 = f32[512,1,4,128]{0,3,2,1:T(8,128)S(1)} fusion(f32[768,512,4]{1,0,2:T(8,128)} %get-tuple-element.364, f32[512,4]{0,1:T(4,128)S(1)} %bitcast.100, pred[512,768]{0,1:T(8,128)(4,1)S(1)} %compare_and_fusion.2, f32[512,1,4,128]{0,3,2,1:T(8,128)S(1)} %get-tuple-element.383, f32[512,4]{0,1:T(4,128)S(1)} %get-tuple-element.365, ...), kind=kOutput, calls=%fused_computation.10.clone.1 | convolution fusion | flops 411303936 | bytes 8994825 | tf_op jit(solution)/shard_map/while/body/eval_jaxpr/rkhn,knd->rkhd/dot_general | solution.py:47
  326.3 1.6 fusion.45
  328.0 0.1 divide_convert_fusion
  328.1 1.0 copy.25
  (63 shorter events, 0.6 us)
Async XLA Ops:
  6.5 0.9 copy-start
  6.5 98.4 %copy-start.2 = (bf16[512,1,512]{2,0,1:T(8,128)(2,1)S(1)}, bf16[512,1,512]{2,0,1:T(8,128)(2,1)}, u32[]{:S(2)}) copy-start(bf16[512,1,512]{2,0,1:T(8,128)(2,1)} %param.11) | copy-start | bytes 1572868
  6.5 98.9 %copy-start.3 = (s32[512,2]{0,1:T(2,128)S(1)}, s32[512,2]{0,1:T(2,128)}, u32[]{:S(2)}) copy-start(s32[512,2]{0,1:T(2,128)} %param.13) | copy-start | bytes 12292
  6.5 223.4 %copy-start.4 = (s32[4]{0:T(128)S(1)}, s32[4]{0:T(128)}, u32[]{:S(2)}) copy-start(s32[4]{0:T(128)} %param.12) | copy-start | bytes 52
  6.5 95.0 %reduce-scatter.2.cloned.1.call-start = ((), (), s32[]{:S(2)}) async-start(), calls=%async_computation.1 | async-start | bytes 884736 | tf_op jit(solution)/shard_map/reduce_scatter | solution.py:59
  11.2 218.7 %all-gather.2.cloned.1.call-start = ((), (), s32[]{:S(2)}) async-start(), calls=%async_computation.2 | async-start | bytes 3194880 | tf_op jit(solution)/shard_map/all_gather | solution.py:84
  235.4 5.2 %copy-start.1 = (f32[768,512,4]{1,0,2:T(8,128)S(1)}, f32[768,512,4]{1,0,2:T(8,128)}, u32[]{:S(2)}) copy-start(f32[768,512,4]{1,0,2:T(8,128)} %get-tuple-element.364) | copy-start | bytes 18874372 | tf_op jit(solution)/shard_map/while
  247.6 5.2 %copy-start.1 = (f32[768,512,4]{1,0,2:T(8,128)S(1)}, f32[768,512,4]{1,0,2:T(8,128)}, u32[]{:S(2)}) copy-start(f32[768,512,4]{1,0,2:T(8,128)} %get-tuple-element.364) | copy-start | bytes 18874372 | tf_op jit(solution)/shard_map/while
  259.9 5.2 %copy-start.1 = (f32[768,512,4]{1,0,2:T(8,128)S(1)}, f32[768,512,4]{1,0,2:T(8,128)}, u32[]{:S(2)}) copy-start(f32[768,512,4]{1,0,2:T(8,128)} %get-tuple-element.364) | copy-start | bytes 18874372 | tf_op jit(solution)/shard_map/while
  272.1 5.2 %copy-start.1 = (f32[768,512,4]{1,0,2:T(8,128)S(1)}, f32[768,512,4]{1,0,2:T(8,128)}, u32[]{:S(2)}) copy-start(f32[768,512,4]{1,0,2:T(8,128)} %get-tuple-element.364) | copy-start | bytes 18874372 | tf_op jit(solution)/shard_map/while
  284.4 5.2 %copy-start.1 = (f32[768,512,4]{1,0,2:T(8,128)S(1)}, f32[768,512,4]{1,0,2:T(8,128)}, u32[]{:S(2)}) copy-start(f32[768,512,4]{1,0,2:T(8,128)} %get-tuple-element.364) | copy-start | bytes 18874372 | tf_op jit(solution)/shard_map/while
  296.6 5.2 %copy-start.1 = (f32[768,512,4]{1,0,2:T(8,128)S(1)}, f32[768,512,4]{1,0,2:T(8,128)}, u32[]{:S(2)}) copy-start(f32[768,512,4]{1,0,2:T(8,128)} %get-tuple-element.364) | copy-start | bytes 18874372 | tf_op jit(solution)/shard_map/while
  308.9 5.2 %copy-start.1 = (f32[768,512,4]{1,0,2:T(8,128)S(1)}, f32[768,512,4]{1,0,2:T(8,128)}, u32[]{:S(2)}) copy-start(f32[768,512,4]{1,0,2:T(8,128)} %get-tuple-element.364) | copy-start | bytes 18874372 | tf_op jit(solution)/shard_map/while
  321.1 5.2 %copy-start.1 = (f32[768,512,4]{1,0,2:T(8,128)S(1)}, f32[768,512,4]{1,0,2:T(8,128)}, u32[]{:S(2)}) copy-start(f32[768,512,4]{1,0,2:T(8,128)} %get-tuple-element.364) | copy-start | bytes 18874372 | tf_op jit(solution)/shard_map/while
Sparse Core Ops, SparseCore 0:
  11.8 89.7 reduce-scatter.1
  105.0 124.9 all-gather.1
where the time goes:
time: 336 us
  waiting for transfers between devices  215 us (64%)
  matrix products  83.5 us (25%)
  other arithmetic  20.1 us (6%)
  between operations  13.5 us (4%)
    all_gather x1, waiting for transfers between devices, shards(): gathered = lax.all_gather(kv_block, ('segment', 'seq'), axis=1, tiled=True)  124 us
    reduce_scatter x1, waiting for transfers between devices, shards(): lax.psum_scatter(jnp.einsum('rd,dch->crh', vision_states, weight_heads, p...  90.3 us
    dot_general x8, matrix products, update(): jnp.einsum('rkhn,knd->rkhd', weights, kv_piece[:, :, head_dim:], preferre...  41.4 us
    dot_general x8, matrix products, update(): jnp.einsum('rkhd,knd->rkhn', query_heads, kv_piece[:, :, :head_dim], pref...  38.4 us
    reduce_sum x8, other arithmetic, update(): row_sum = row_sum * factor + jnp.sum(expterm, axis=-1)  12.6 us
  transfers between devices with their start and end apart: 2, of which 2 were waited for; matrix products, arithmetic and copies ran while one was open for 0% of the time, Pallas kernels for 0%

commit v1 on v0

v1 whole, which is shorter than its diff:
```python
import functools
import math

import jax
import jax.numpy as jnp
from jax import lax
from jax.experimental import pallas as pl
from jax.experimental.pallas import tpu as pltpu
from jax.sharding import PartitionSpec as P

MESH = pl.DeviceIdType.MESH
F32 = jnp.float32
BF16 = jnp.bfloat16
NEG = -1e30
SUB = 32
RING = 32
ORDER = ((0, 1), (0, 2), (1, 2), (1, 3), (0, 3), (0, 4), (1, 4), (2, 4), (2, 3), (3, 4))


def project_gather(
    nz, vis_ref, w_ref, gain_ref, q_ref, tt_ref,
    kv_ref, qs_ref, pt_ref, lohi_ref, flag_ref,
    w_buf, part_out, part_in, w_sem, rs_send, rs_recv,
    a_send, a_recv, b_send, b_recv, x_send, x_recv, n_send, n_recv, ca_send, ca_recv, cn_send, cn_recv,
):
    heads = w_buf.shape[0]
    hd = gain_ref.shape[1]
    width = 2 * hd
    rows = vis_ref.shape[0]
    seg = lax.axis_index("segment")
    seq = lax.axis_index("seq")
    ten = lax.axis_index("tensor")
    z, core = seq // 2, seq % 2
    up, down = (z + 1) % nz, (z + nz - 1) % nz
    to_up = {"seq": up * 2 + core}
    to_down = {"seq": down * 2 + core}
    to_x = {"segment": 1 - seg}
    to_core = {"seq": z * 2 + (1 - core)}

    def weight_copy(k):
        head = (ten + k) % heads
        cols = pl.ds(pl.multiple_of(head * width, width), width)
        return pltpu.make_async_copy(w_ref.at[:, cols], w_buf.at[k], w_sem.at[k])

    order = list(range(1, heads)) + [0]
    for k in order:
        weight_copy(k).start()

    barrier = pltpu.get_barrier_semaphore()
    for k in range(1, heads):
        pl.semaphore_signal(barrier, inc=1, device_id={"tensor": (ten + k) % heads}, device_id_type=MESH)
    for target in (to_up, to_down, to_x, to_core):
        pl.semaphore_signal(barrier, inc=1, device_id=target, device_id_type=MESH)
    pl.semaphore_wait(barrier, heads + 3)

    def partial_copy(k):
        return pltpu.make_async_remote_copy(
            src_ref=part_out.at[k], dst_ref=part_in.at[k], send_sem=rs_send.at[k], recv_sem=rs_recv.at[k],
            device_id={"tensor": (ten + k) % heads}, device_id_type=MESH,
        )

    for k in order:
        weight_copy(k).wait()
        part_out[k] = jnp.dot(vis_ref[...], w_buf[k], preferred_element_type=F32)
        if k:
            partial_copy(k).start()

    count = tt_ref.shape[1]
    low_row = tt_ref[0:1, :].astype(F32)
    high_row = tt_ref[1:2, :].astype(F32)
    rank_row = jnp.full_like(low_row, float(len(ORDER)))
    for place, (first, last) in enumerate(ORDER):
        rank_row = jnp.where((low_row == first) & (high_row == last), float(place), rank_row)
    row_id = lax.broadcasted_iota(jnp.int32, (count, count), 0)
    col_id = lax.broadcasted_iota(jnp.int32, (count, count), 1)
    here = row_id == col_id

    def column(row):
        return jnp.sum(jnp.where(here, row, 0.0), axis=1, keepdims=True)

    key_row = rank_row
    key_col = column(rank_row)
    ahead_row = (key_col < key_row) | ((key_col == key_row) & (row_id < col_id))
    place_row = jnp.sum(jnp.where(ahead_row, 1.0, 0.0), axis=0, keepdims=True)
    ahead_col = (key_row < key_col) | ((key_row == key_col) & (col_id < row_id))
    place_col = jnp.sum(jnp.where(ahead_col, 1.0, 0.0), axis=1, keepdims=True)
    perm = row_id.astype(F32) == place_row
    pt_ref[...] = jnp.where(col_id.astype(F32) == place_col, 1.0, 0.0).astype(BF16)
    qs_ref[...] = jnp.dot(
        jnp.where(perm, 1.0, 0.0).astype(BF16), q_ref[...], preferred_element_type=F32
    ).astype(BF16)
    low_sorted = jnp.sum(jnp.where(perm, low_row, 0.0), axis=1, keepdims=True)
    high_sorted = jnp.sum(jnp.where(perm, high_row, 0.0), axis=1, keepdims=True)
    lane = lax.broadcasted_iota(jnp.int32, (count, 128), 1)
    lohi_ref[...] = jnp.where(lane == 0, low_sorted, high_sorted)
    lane_f = lane.astype(F32)
    sees = jnp.where((low_sorted <= lane_f) & (lane_f < high_sorted), 1.0, 0.0)
    for block in range(count // SUB):
        flag_ref[block : block + 1, :] = jnp.max(
            sees[block * SUB : (block + 1) * SUB], axis=0, keepdims=True
        ).astype(jnp.int32)

    total = part_out[0]
    for k in range(1, heads):
        partial_copy(k).wait_recv()
        total = total + part_in[k]
    keys_raw = total[:, :hd]
    mean_sq = jnp.mean(keys_raw * keys_raw, axis=-1, keepdims=True)
    normed = keys_raw * lax.rsqrt(mean_sq + 1e-05) * gain_ref[...]

    def slot(segment, zz, cc):
        return segment * (2 * nz) + zz * 2 + cc

    mine = slot(seg, z, core)
    kv_ref[mine, :, :hd] = normed.astype(BF16)
    kv_ref[mine, :, hd:] = total[:, hd:].astype(BF16)

    def move(block, first, size, send, recv, target):
        piece = kv_ref.at[block, pl.ds(first, size)]
        return pltpu.make_async_remote_copy(
            src_ref=piece, dst_ref=piece, send_sem=send, recv_sem=recv, device_id=target, device_id_type=MESH
        )

    def ring_a(way, d, target):
        zz = (z + nz - d) % nz if way == 0 else (z + d) % nz
        return move(slot(seg, zz, core), 0, rows, a_send.at[way, d], a_recv.at[way, d], target)

    def ring_b(way, d, target):
        zz = (z + nz - d) % nz if way == 0 else (z + d) % nz
        return move(slot(1 - seg, zz, core), 0, RING, b_send.at[way, d], b_recv.at[way, d], target)

    def send_a(way, d):
        zz = (z + nz - d) % nz if way == 0 else (z + d) % nz
        return move(
            slot(seg, zz, core), 0, rows, a_send.at[way, d], a_recv.at[way, d + 1], to_up if way == 0 else to_down
        )

    def send_b(way, d):
        zz = (z + nz - d) % nz if way == 0 else (z + d) % nz
        return move(
            slot(1 - seg, zz, core), 0, RING, b_send.at[way, d], b_recv.at[way, d + 1], to_up if way == 0 else to_down
        )

    def x_copy(zz, mine_side):
        side = seg if mine_side else 1 - seg
        off = (zz + nz - z) % nz
        return move(slot(side, zz, core), RING, rows - RING, x_send.at[off], x_recv.at[off], to_x)

    def nb_copy(mine_side):
        side = seg if mine_side else 1 - seg
        return move(slot(side, z, core), 0, RING, n_send, n_recv, to_x)

    def core_copy(zz, own_column, outgoing):
        side = seg if own_column else 1 - seg
        off = (zz + nz - z) % nz
        send, recv = (ca_send, ca_recv) if own_column else (cn_send, cn_recv)
        cc = core if outgoing else 1 - core
        return move(slot(side, zz, cc), 0, rows, send.at[off], recv.at[off], to_core)

    half = nz // 2

    nb_copy(True).start()
    send_a(0, 0).start()
    send_a(1, 0).start()
    x_copy(z, True).start()
    nb_copy(False).wait_recv()
    send_b(0, 0).start()
    send_b(1, 0).start()
    core_copy(z, True, True).start()

    def hop(d, carry):
        above = (z + nz - d) % nz
        below = (z + d) % nz
        ring_a(0, d, to_up).wait_recv()
        send_a(0, d).start()
        ring_a(1, d, to_down).wait_recv()

        @pl.when(d < half - 1)
        def _():
            send_a(1, d).start()

        x_copy(above, True).start()
        x_copy(below, True).start()
        ring_b(0, d, to_up).wait_recv()

        @pl.when(d < half - 1)
        def _():
            send_b(0, d).start()

        ring_b(1, d, to_down).wait_recv()
        send_b(1, d).start()
        core_copy(above, True, True).start()
        core_copy(below, True, True).start()
        last = (z + nz - d + 1) % nz
        x_copy(last, False).wait_recv()
        core_copy(last, False, True).start()

        @pl.when(d > 1)
        def _():
            other = (z + d - 1) % nz
            x_copy(other, False).wait_recv()
            core_copy(other, False, True).start()

        return carry

    lax.fori_loop(1, half, hop, 0)
    far = (z + half) % nz
    ring_a(0, half, to_up).wait_recv()
    x_copy(far, True).start()
    core_copy(far, True, True).start()
    ring_b(1, half, to_down).wait_recv()
    for zz in ((z + half + 1) % nz, (z + half - 1) % nz, far):
        x_copy(zz, False).wait_recv()
        core_copy(zz, False, True).start()

    def finish(off, carry):
        zz = (z + off) % nz
        core_copy(zz, True, False).wait_recv()
        core_copy(zz, False, False).wait_recv()
        core_copy(zz, True, True).wait_send()
        core_copy(zz, False, True).wait_send()
        x_copy(zz, True).wait_send()
        return carry

    lax.fori_loop(0, nz, finish, 0)
    nb_copy(True).wait_send()
    for k in range(1, heads):
        partial_copy(k).wait_send()

    def finish_ring(d, carry):
        send_a(0, d).wait_send()
        send_b(1, d).wait_send()

        @pl.when(d < half - 1)
        def _():
            send_a(1, d).wait_send()
            send_b(0, d).wait_send()

        return carry

    lax.fori_loop(0, half, finish_ring, 0)


def attend(
    scale, tile_len, least, tokens_ref, flag_ref, kv_ref, qs_ref, pt_ref, lohi_ref, out_ref,
    acc, top, low_sum, sorted_out, blocks_of, *, group=2,
):
    tiles = kv_ref.shape[0] // tile_len
    hd = kv_ref.shape[1] // 2
    count = qs_ref.shape[0] // SUB
    heads = qs_ref.shape[1] // hd
    chunk = 256
    acc[...] = jnp.zeros_like(acc)
    low_sum[...] = jnp.zeros_like(low_sum)
    top[...] = jnp.full_like(top, NEG)
    factor = scale * math.log2(math.e)

    def visit(tile, n_chunks, masked, picked, valid):
        rows_of = []
        for block in picked:
            src = pl.multiple_of(jnp.where(block == count, 0, block) * SUB, SUB)
            for h in range(heads):
                rows_of.append(qs_ref[pl.ds(src, SUB), h * hd : (h + 1) * hd])
        q = jnp.concatenate(rows_of, axis=0)
        scores = []
        for c in range(n_chunks):
            at = pl.multiple_of(tile * tile_len + c * chunk, chunk)
            s = lax.dot_general(
                q, kv_ref[pl.ds(at, chunk), :hd], (((1,), (1,)), ((), ())), preferred_element_type=F32
            )
            if masked and c == n_chunks - 1:
                lane = lax.broadcasted_iota(jnp.int32, s.shape, 1)
                s = jnp.where(lane < valid - c * chunk, s, NEG)
            scores.append(s)
        best = scores[0]
        for s in scores[1:]:
            best = jnp.maximum(best, s)
        peak = jnp.max(best, axis=1, keepdims=True)
        part = None
        summed = None
        for c, s in enumerate(scores):
            at = pl.multiple_of(tile * tile_len + c * chunk, chunk)
            e = jnp.exp2((s - peak) * factor)
            part = e if part is None else part + e
            o = jnp.dot(e.astype(BF16), kv_ref[pl.ds(at, chunk), hd:], preferred_element_type=F32)
            summed = o if summed is None else summed + o
        row_sum = jnp.sum(part, axis=1, keepdims=True)
        span = heads * SUB
        for i, block in enumerate(picked):
            src = pl.multiple_of(jnp.where(block == count, 0, block) * SUB, SUB)
            low = lohi_ref[pl.ds(src, SUB), 0:1]
            high = lohi_ref[pl.ds(src, SUB), 1:2]
            tile_f = tile.astype(F32)
            seen = jnp.where((low <= tile_f) & (tile_f < high), 1.0, 0.0)
            seen = jnp.concatenate([seen] * heads, axis=0)
            part_slice = slice(i * span, (i + 1) * span)
            mine = jnp.where(seen > 0.0, peak[part_slice], NEG)
            old = top[block]
            new = jnp.maximum(old, mine)
            keep = jnp.exp2((old - new) * factor)
            take = jnp.where(seen > 0.0, jnp.exp2((mine - new) * factor), 0.0)
            top[block] = new
            low_sum[block] = low_sum[block] * keep + row_sum[part_slice] * take
            acc[block] = acc[block] * keep + summed[part_slice] * take

    def one_tile(tile, carry):
        def collect(block, found):
            blocks_of[found] = block
            return found + flag_ref[block, tile]

        found = lax.fori_loop(0, count, collect, 0)
        for i in range(group - 1):
            blocks_of[found + i] = count
        trips = (found + group - 1) // group
        valid = tokens_ref[tile]
        base = least // chunk
        extra = (valid - least + chunk - 1) // chunk
        for more in range((tile_len - least) // chunk + 1):

            @pl.when(extra == more)
            def _(more=more):
                def pair(i, c):
                    visit(tile, base + more, more > 0, [blocks_of[i * group + j] for j in range(group)], valid)
                    return c

                lax.fori_loop(0, trips, pair, 0)

        return carry

    lax.fori_loop(0, tiles, one_tile, 0)

    def close(block, carry):
        src = pl.multiple_of(block * SUB, SUB)
        low = lohi_ref[pl.ds(src, SUB), 0:1]
        high = lohi_ref[pl.ds(src, SUB), 1:2]
        unseen = jnp.where(high <= low, 1.0, 0.0)
        unseen = jnp.concatenate([unseen] * heads, axis=0)
        done = (acc[block] / (low_sum[block] + unseen)).astype(BF16)
        for h in range(heads):
            sorted_out[pl.ds(src, SUB), h * hd : (h + 1) * hd] = done[h * SUB : (h + 1) * SUB]
        return carry

    lax.fori_loop(0, count, close, 0)
    out_ref[...] = jnp.dot(pt_ref[...], sorted_out[...], preferred_element_type=F32).astype(BF16)


def run_attend(tile_tokens, flags, kv, qs, pt, lohi, head_dim):
    text_rows, cols = qs.shape
    tile_len = kv.shape[0] // tile_tokens.shape[0]
    span = (cols // head_dim) * SUB
    blocks = text_rows // SUB
    smem = pl.BlockSpec(memory_space=pltpu.SMEM)
    vmem = pl.BlockSpec(memory_space=pltpu.VMEM)
    return pl.pallas_call(
        functools.partial(attend, head_dim ** (-0.5), tile_len, tile_len // 2),
        out_shape=jax.ShapeDtypeStruct((text_rows, cols), BF16),
        in_specs=[smem, smem, vmem, vmem, vmem, vmem],
        out_specs=vmem,
        scratch_shapes=[
            pltpu.VMEM((blocks + 1, span, head_dim), F32),
            pltpu.VMEM((blocks + 1, span, head_dim), F32),
            pltpu.VMEM((blocks + 1, span, head_dim), F32),
            pltpu.VMEM((text_rows, cols), BF16),
            pltpu.SMEM((blocks + 8,), jnp.int32),
        ],
        compiler_params=pltpu.CompilerParams(vmem_limit_bytes=40 << 20),
        name="attend",
    )(tile_tokens, flags, kv, qs, pt, lohi)


def shards(vision_states, kv_weight, key_gain, queries, tile_tokens, text_tiles):
    head_dim = key_gain.shape[0]
    rows = vision_states.shape[0]
    heads = lax.axis_size("tensor")
    nz = lax.axis_size("seq") // 2
    pieces = lax.axis_size("segment") * lax.axis_size("seq")
    depth = vision_states.shape[1]
    text_rows = queries.shape[0]
    q = queries.reshape(text_rows, queries.shape[2])
    vmem = pl.BlockSpec(memory_space=pltpu.VMEM)
    dma = pltpu.SemaphoreType.DMA
    kv, qs, pt, lohi, flags = pl.pallas_call(
        functools.partial(project_gather, nz),
        out_shape=(
            jax.ShapeDtypeStruct((pieces, rows, 2 * head_dim), BF16),
            jax.ShapeDtypeStruct(q.shape, BF16),
            jax.ShapeDtypeStruct((text_rows, text_rows), BF16),
            jax.ShapeDtypeStruct((text_rows, 128), F32),
            jax.ShapeDtypeStruct((text_rows // SUB, 128), jnp.int32),
        ),
        in_specs=[vmem, pl.BlockSpec(memory_space=pl.ANY), vmem, vmem, vmem],
        out_specs=(vmem,) * 5,
        scratch_shapes=[
            pltpu.VMEM((heads, depth, 2 * head_dim), BF16),
            pltpu.VMEM((heads, rows, 2 * head_dim), F32),
            pltpu.VMEM((heads, rows, 2 * head_dim), F32),
            dma((heads,)), dma((heads,)), dma((heads,)),
            dma((2, nz // 2 + 1)), dma((2, nz // 2 + 1)), dma((2, nz // 2 + 1)), dma((2, nz // 2 + 1)),
            dma((nz,)), dma((nz,)), dma, dma,
            dma((nz,)), dma((nz,)), dma((nz,)), dma((nz,)),
        ],
        compiler_params=pltpu.CompilerParams(
            collective_id=0, has_side_effects=True, vmem_limit_bytes=40 << 20
        ),
        name="project_gather",
    )(vision_states, kv_weight, key_gain.reshape(1, head_dim), q, text_tiles.T)
    kv = kv.reshape(pieces * rows, 2 * head_dim)
    out = run_attend(tile_tokens, flags, kv, qs, pt, lohi, head_dim)
    return out.reshape(queries.shape)


def solution(mesh):
    placed = (
        P(("segment", "seq"), "tensor"),
        P("tensor", None),
        P(),
        P("seq", "tensor", "segment"),
        P(),
        P("seq", None),
    )
    return jax.shard_map(
        shards, mesh=mesh, in_specs=placed, out_specs=P("seq", "tensor", "segment"), check_vma=False
    )
```

time: 336 us -> 86.1 us (0.26)
  waiting for transfers between devices: 215 us -> 0 us
  matrix products: 83.5 us -> 0 us
  Pallas kernels: 0 us -> 80.4 us
  other arithmetic: 20.1 us -> 0 us
  between operations: 13.5 us -> 0.02 us
    all_gather x1 -> x0, waiting for transfers between devices: 124 us -> none  [shards(): gathered = lax.all_gather(kv_block, ('segment', 'seq'), axis=1, tiled=True)]
    reduce_scatter x1 -> x0, waiting for transfers between devices: 90.3 us -> none  [shards(): lax.psum_scatter(jnp.einsum('rd,dch->crh', vision_states, weight_heads, p...]
    dot_general x17 -> x0, matrix products: 83.5 us -> none  [the longest x8 41.4 us: update(): jnp.einsum('rkhn,knd->rkhd', weights, kv_piece[:, :, head_dim:], preferre...]
    pallas_call x0 -> x2, Pallas kernels: none -> 80.4 us  [the longest x1 60.2 us: shards(): pl.pallas_call(functools.partial(project_gather, nz), out_shape=(jax.Shap...]
    reduce_sum x17 -> x0, other arithmetic: 14.1 us -> none  [the longest x8 12.6 us: update(): row_sum = row_sum * factor + jnp.sum(expterm, axis=-1)]
    unnamed x10 -> x12, local copies, waits for them, and re-layouts: 1.42 us -> 5.44 us
    and x8 -> x0, other arithmetic: 3.81 us -> none  [visibility(): key_valid[None, :] & (tile_ids[None, :] >= lower[:, None])]
  transfers between devices with their start and end apart: 2 -> 0, of which waited for: 2 -> 0; matrix products, arithmetic and copies ran while one was open for 0% -> 0% of each run, Pallas kernels for 0% -> 0%
where the time goes in v1:
time: 86.1 us; the launch traced here: 85.8 us
  Pallas kernels  80.4 us (93%)
  local copies, waits for them, and re-layouts  5.44 us (6%)
    pallas_call x1, Pallas kernels, shards(): pl.pallas_call(functools.partial(project_gather, nz), out_shape=(jax.Shap...  60.2 us
    pallas_call x1, Pallas kernels, run_attend(): pl.pallas_call(functools.partial(attend, head_dim ** (-0.5), tile_len, ti...  20.1 us
    unnamed x12, local copies, waits for them, and re-layouts  5.44 us

profile of v1, /device:TPU:1, one launch (start us, length us, event | category | flops | bytes accessed | tf_op | source)
XLA Modules:
  0.0 85.8 jit_solution(12947399227762418338)
XLA Ops:
  0.0 0.0 copy-start.5
  0.0 0.0 copy-start
  0.0 2.1 %copy-done = bf16[960,2048]{1,0:T(8,128)(2,1)S(1)} copy-done((bf16[960,2048]{1,0:T(8,128)(2,1)S(1)}, bf16[960,2048]{1,0:T(8,128)(2,1)}, u32[]{:S(2)}) %copy-start) | copy-done | bytes 3932184
  2.1 0.0 copy-start.1
  2.1 1.0 %copy-done.1 = bf16[512,1,512]{2,0,1:T(8,128)(2,1)S(1)} copy-done((bf16[512,1,512]{2,0,1:T(8,128)(2,1)S(1)}, bf16[512,1,512]{2,0,1:T(8,128)(2,1)}, u32[]{:S(2)}) %copy-start.1) | copy-done | bytes 524312
  3.2 0.0 copy-start.2
  3.2 0.9 %copy-done.2 = bf16[96,960]{1,0:T(8,128)(2,1)S(1)} copy-done((bf16[96,960]{1,0:T(8,128)(2,1)S(1)}, bf16[96,960]{1,0:T(8,128)(2,1)}, u32[]{:S(2)}) %copy-start.2) | copy-done | bytes 184344
  4.1 0.0 copy-start.3
  4.1 0.7 copy-done.3
  4.8 0.0 copy-start.4
  4.8 0.7 copy-done.4
  5.4 60.2 %project_gather.1 = (bf16[64,96,256]{2,1,0:T(8,128)(2,1)S(1)}, bf16[512,512]{1,0:T(8,128)(2,1)S(1)}, bf16[512,512]{1,0:T(8,128)(2,1)S(1)}, f32[512,128]{1,0:T(8,128)S(1)}, s32[16,128]{1,0:T(8,128)S(1)}) custom-call(bf16[96,960]{1,0:T(8,128)(2,1)S(1)} %copy-done.2, bf16[960,2048]{1,0:T(8,128)(2,1)S(1)} %copy-done, f32[1,128]{1,0:T(1,128)S(1)} %bitcast.8, ...), custom_call_target="tpu_custom_call" | custom-call | tf_op jit(solution)/shard_map/project_gather/pallas_call | solution.py:382
  65.7 0.0 copy-done.5
  65.7 20.1 %attend.1 = bf16[512,512]{1,0:T(8,128)(2,1)} custom-call(s32[4]{0:T(128)S(1)} %copy-done.5, s32[16,128]{1,0:T(8,128)S(1)} %get-tuple-element.10.flag_ref, bf16[6144,256]{1,0:T(8,128)(2,1)S(1)} %bitcast.5, bf16[512,512]{1,0:T(8,128)(2,1)S(1)} %get-tuple-element.12.qs_ref, bf16[512,512]{1,0:T(8,128)(2,1)S(1)} %get-tuple-element.13.pt_ref, ...), custom_call_target="tpu_custom_call" | custom-call | tf_op jit(solution)/shard_map/attend/pallas_call | solution.py:354
Async XLA Ops:
  0.0 65.7 %copy-start.5 = (s32[4]{0:T(128)S(1)}, s32[4]{0:T(128)}, u32[]{:S(2)}) copy-start(s32[4]{0:T(128)} %tokens_ref.1) | copy-start | bytes 52
  0.0 2.1 %copy-start = (bf16[960,2048]{1,0:T(8,128)(2,1)S(1)}, bf16[960,2048]{1,0:T(8,128)(2,1)}, u32[]{:S(2)}) copy-start(bf16[960,2048]{1,0:T(8,128)(2,1)} %w_ref.1) | copy-start | bytes 11796484
  2.1 1.0 %copy-start.1 = (bf16[512,1,512]{2,0,1:T(8,128)(2,1)S(1)}, bf16[512,1,512]{2,0,1:T(8,128)(2,1)}, u32[]{:S(2)}) copy-start(bf16[512,1,512]{2,0,1:T(8,128)(2,1)} %param.9) | copy-start | bytes 1572868
  3.2 0.9 %copy-start.2 = (bf16[96,960]{1,0:T(8,128)(2,1)S(1)}, bf16[96,960]{1,0:T(8,128)(2,1)}, u32[]{:S(2)}) copy-start(bf16[96,960]{1,0:T(8,128)(2,1)} %vis_ref.1) | copy-start | bytes 552964
  4.1 0.7 copy-start.3
  4.8 0.7 copy-start.4

commit v2 on v1

v2 whole, which is shorter than its diff:
```python
import functools
import math

import jax
import jax.numpy as jnp
from jax import lax
from jax.experimental import pallas as pl
from jax.experimental.pallas import tpu as pltpu
from jax.sharding import PartitionSpec as P

MESH = pl.DeviceIdType.MESH
F32 = jnp.float32
BF16 = jnp.bfloat16
NEG = -1e30
SUB = 16
TREE = {2: 0, 4: 2, 6: 4, 8: 6, 1: 0, 3: 2, 5: 4, 7: 6}
ARRIVAL = (2, 1, 4, 3, 6, 5, 8, 7)
LAG = 6
BLAG = 1
RING = 16
VALUE_PART = BF16
ORDER = ((0, 1), (0, 2), (1, 2), (1, 3), (0, 3), (0, 4), (1, 4), (2, 4), (2, 3), (3, 4))


def project_gather(
    nz, vis_hbm, w_hbm, gain_hbm, q_hbm, tt_hbm,
    kv_ref, qs_ref, pt_ref, lohi_ref, flag_ref,
    vis_ref, w_ref, gain_ref, q_ref, tt_ref, key_out, key_in, value_out, value_in, mine_part,
    in_sem, w_sem, rs_send, rs_recv, a_recv, b_recv, x_recv, n_recv, core_recv, sent,
):
    heads = w_ref.shape[0]
    hd = gain_ref.shape[1]
    width = 2 * hd
    rows = vis_ref.shape[0]
    seg = lax.axis_index("segment")
    seq = lax.axis_index("seq")
    ten = lax.axis_index("tensor")
    z, core = seq // 2, seq % 2
    to_x = {"segment": 1 - seg}
    to_core = {"seq": z * 2 + (1 - core)}

    inputs = [
        pltpu.make_async_copy(src, dst, in_sem.at[n])
        for n, (src, dst) in enumerate(
            ((vis_hbm, vis_ref), (gain_hbm, gain_ref), (q_hbm, q_ref), (tt_hbm, tt_ref))
        )
    ]

    def weight_copy(k):
        head = (ten + k) % heads
        cols = pl.ds(pl.multiple_of(head * width, width), width)
        return pltpu.make_async_copy(w_hbm.at[:, cols], w_ref.at[k], w_sem.at[k])

    order = list(range(1, heads)) + [0]
    inputs[0].start()
    for k in order:
        weight_copy(k).start()
    for copy in inputs[1:]:
        copy.start()

    barrier = pltpu.get_barrier_semaphore()
    for k in range(1, heads):
        pl.semaphore_signal(barrier, inc=1, device_id={"tensor": (ten + k) % heads}, device_id_type=MESH)
    near = sorted({d - held for d, held in TREE.items()})
    near = [{"seq": (z + hop) % nz * 2 + core} for jump in near for hop in (jump, nz - jump)]
    for target in near + [to_x, to_core]:
        pl.semaphore_signal(barrier, inc=1, device_id=target, device_id_type=MESH)

    def partial_copy(k, n):
        out, into = ((key_out, key_in), (value_out, value_in))[n]
        return pltpu.make_async_remote_copy(
            src_ref=out.at[k - 1], dst_ref=into.at[k - 1], send_sem=rs_send.at[n], recv_sem=rs_recv.at[n],
            device_id={"tensor": (ten + k) % heads}, device_id_type=MESH,
        )

    inputs[0].wait()
    for k in order:
        weight_copy(k).wait()
        part = jnp.dot(vis_ref[...], w_ref[k], preferred_element_type=F32)
        if k:
            key_out[k - 1] = part[:, :hd].astype(key_out.dtype)
            value_out[k - 1] = part[:, hd:].astype(value_out.dtype)
            if k == 1:
                pl.semaphore_wait(barrier, heads - 1 + len(near) + 2)
            partial_copy(k, 0).start()
            partial_copy(k, 1).start()
        else:
            mine_part[...] = part

    for copy in inputs[1:]:
        copy.wait()
    count = tt_ref.shape[1]
    low_row = tt_ref[0:1, :].astype(F32)
    high_row = tt_ref[1:2, :].astype(F32)
    key_row = jnp.full_like(low_row, float(len(ORDER)))
    for place, (first, last) in enumerate(ORDER):
        key_row = jnp.where((low_row == first) & (high_row == last), float(place), key_row)
    row_id = lax.broadcasted_iota(jnp.int32, (count, count), 0)
    col_id = lax.broadcasted_iota(jnp.int32, (count, count), 1)
    key_col = jnp.sum(jnp.where(row_id == col_id, key_row, 0.0), axis=1, keepdims=True)
    ahead_row = (key_col < key_row) | ((key_col == key_row) & (row_id < col_id))
    place_row = jnp.sum(jnp.where(ahead_row, 1.0, 0.0), axis=0, keepdims=True)
    ahead_col = (key_row < key_col) | ((key_row == key_col) & (col_id < row_id))
    place_col = jnp.sum(jnp.where(ahead_col, 1.0, 0.0), axis=1, keepdims=True)
    perm = row_id.astype(F32) == place_row
    pt_ref[...] = jnp.where(col_id.astype(F32) == place_col, 1.0, 0.0).astype(BF16)
    qs_ref[...] = jnp.dot(
        jnp.where(perm, 1.0, 0.0).astype(BF16), q_ref[...], preferred_element_type=F32
    ).astype(BF16)
    low_sorted = jnp.sum(jnp.where(perm, low_row, 0.0), axis=1, keepdims=True)
    high_sorted = jnp.sum(jnp.where(perm, high_row, 0.0), axis=1, keepdims=True)
    lane = lax.broadcasted_iota(jnp.int32, (count, 128), 1)
    lohi_ref[:, :hd] = jnp.broadcast_to(low_sorted, (count, hd))
    lohi_ref[:, hd:] = jnp.broadcast_to(high_sorted, (count, hd))
    lane_f = lane.astype(F32)
    sees = jnp.where((low_sorted <= lane_f) & (lane_f < high_sorted), 1.0, 0.0)
    for block in range(count // SUB):
        flag_ref[block : block + 1, :] = jnp.max(
            sees[block * SUB : (block + 1) * SUB], axis=0, keepdims=True
        ).astype(jnp.int32)

    def all_of(ref, sem):
        pltpu.make_async_copy(ref, ref, sem).wait()

    all_of(key_in, rs_recv.at[0])
    keys_raw = mine_part[:, :hd]
    for k in range(heads - 1):
        keys_raw = keys_raw + key_in[k].astype(F32)
    mean_sq = jnp.mean(keys_raw * keys_raw, axis=-1, keepdims=True)
    normed = keys_raw * lax.rsqrt(mean_sq + 1e-05) * gain_ref[...]

    def slot(segment, zz, cc):
        return segment * (2 * nz) + zz * 2 + cc

    mine = slot(seg, z, core)
    kv_ref[mine, :, :hd] = normed.astype(BF16)
    all_of(value_in, rs_recv.at[1])
    values_raw = mine_part[:, hd:]
    for k in range(heads - 1):
        values_raw = values_raw + value_in[k].astype(F32)
    kv_ref[mine, :, hd:] = values_raw.astype(BF16)

    sends = [0]

    def move(block, first, size, recv, target):
        piece = kv_ref.at[block, pl.ds(first, size)]
        return pltpu.make_async_remote_copy(
            src_ref=piece, dst_ref=piece, send_sem=sent, recv_sem=recv, device_id=target, device_id_type=MESH
        )

    def go(copy, size):
        sends[0] += size
        copy.start()

    half = nz // 2

    def place(way, d):
        return (z + nz - d) % nz if way == 0 else (z + d) % nz

    def ahead(way, d):
        jump = d - TREE[d]
        hop = jump if way == 0 else nz - jump
        return {"seq": (z + hop) % nz * 2 + core}

    def span_a(way, d):
        return (way * (rows // 2), rows // 2) if d == half else (0, rows)

    def copy_a(way, held, d):
        return move(slot(seg, place(way, held), core), *span_a(way, d), a_recv.at[way, d - 1], ahead(way, d))

    def copy_b(way, held, d):
        return move(slot(1 - seg, place(way, held), core), 0, RING, b_recv.at[way, d - 1], ahead(way, d))

    def comes_b(way, d):
        return d < half or way == 1

    def span_x(way, d):
        first, size = span_a(way, d)
        last = first + size
        first = max(first, RING)
        return first, last - first

    def cross(way, d):
        first, size = span_x(way, d)
        go(move(slot(seg, place(way, d), core), first, size, x_recv.at[way, d], to_x), size)

    def crossed(way, d):
        move(slot(1 - seg, place(way, d), core), *span_x(way, d), x_recv.at[way, d], to_x).wait_recv()

    def swap(side, way, d):
        go(move(slot(side, place(way, d), core), 0, rows, core_recv, to_core), rows)

    def on_a(way, held):
        for d in TREE:
            if TREE[d] == held:
                go(copy_a(way, held, d), span_a(way, d)[1])

    def on_b(way, held):
        for d in TREE:
            if TREE[d] == held and comes_b(way, d):
                go(copy_b(way, held, d), RING)

    both = (0, 1)
    go(move(mine, 0, RING, n_recv, to_x), RING)
    for way in both:
        on_a(way, 0)
    cross(0, 0)
    swap(seg, 0, 0)
    move(slot(1 - seg, z, core), 0, RING, n_recv, to_x).wait_recv()
    for way in both:
        on_b(way, 0)
    waiting = [(0, 0)]

    def take_crossed(keep):
        while len(waiting) > keep:
            way, d = waiting.pop(0)
            crossed(way, d)
            if d < half or way == 1:
                swap(1 - seg, way, d)

    late = []

    def take_b(keep):
        while len(late) > keep:
            d = late.pop(0)
            for way in both:
                if comes_b(way, d):
                    copy_b(way, d, d).wait_recv()
                    on_b(way, d)

    for d in ARRIVAL:
        for way in both:
            copy_a(way, d, d).wait_recv()
            on_a(way, d)
        for way in both:
            cross(way, d)
        late.append(d)
        take_b(BLAG)
        for way in both:
            if d < half or way == 1:
                swap(seg, way, d)
        take_crossed(LAG)
        waiting += [(0, d), (1, d)]
    take_b(0)
    take_crossed(0)

    all_of(kv_ref.at[pl.ds(0, 2 * nz)], core_recv)
    assert sends[0] % rows == 0
    all_of(kv_ref.at[pl.ds(0, sends[0] // rows)], sent)
    all_of(key_out, rs_send.at[0])
    all_of(value_out, rs_send.at[1])


def attend(
    scale, tile_len, least, tokens_ref, flag_ref, kv_ref, qs_ref, pt_ref, lohi_ref, out_ref,
    acc, top, low_sum, sorted_out, s_ref, peak_ref, blocks_of, *, group=4,
):
    tiles = kv_ref.shape[0] // tile_len
    hd = kv_ref.shape[1] // 2
    count = qs_ref.shape[0] // SUB
    heads = qs_ref.shape[1] // hd
    chunk = 256
    acc[...] = jnp.zeros_like(acc)
    low_sum[...] = jnp.zeros_like(low_sum)
    top[...] = jnp.full_like(top, NEG)
    factor = scale * math.log2(math.e)

    def queries_of(picked):
        rows_of = []
        for block in picked:
            src = pl.multiple_of(jnp.where(block == count, 0, block) * SUB, SUB)
            for h in range(heads):
                rows_of.append(qs_ref[pl.ds(src, SUB), h * hd : (h + 1) * hd])
        return jnp.concatenate(rows_of, axis=0)

    def score(tile, c, n_chunks, q, valid):
        at = pl.multiple_of(tile * tile_len + c * chunk, chunk)
        s = lax.dot_general(
            q, kv_ref[pl.ds(at, chunk), :hd], (((1,), (1,)), ((), ())), preferred_element_type=F32
        )
        if c == n_chunks - 1 and c * chunk >= least:
            lane = lax.broadcasted_iota(jnp.int32, s.shape, 1)
            s = jnp.where(lane < valid - c * chunk, s, NEG)
        return s

    def step(tile, n_chunks, picked, following, valid):
        q = None if following is None else queries_of(following)
        peak = peak_ref[...]
        part = summed = best = None
        for c in range(n_chunks):
            cols = slice(c * chunk, (c + 1) * chunk)
            at = pl.multiple_of(tile * tile_len + c * chunk, chunk)
            old = s_ref[:, cols]
            s = None if q is None else score(tile, c, n_chunks, q, valid)
            halves = [
                jnp.exp2((old[:, x : x + hd] - peak) * factor) for x in range(0, chunk, hd)
            ]
            for e in halves:
                part = e if part is None else part + e
            e16 = jnp.concatenate([e.astype(BF16) for e in halves], axis=1)
            o = jnp.dot(e16, kv_ref[pl.ds(at, chunk), hd:], preferred_element_type=F32)
            summed = o if summed is None else summed + o
            if s is not None:
                s_ref[:, cols] = s
                fold = jnp.maximum(s[:, :hd], s[:, hd:])
                best = fold if best is None else jnp.maximum(best, fold)
        high = part.astype(BF16)
        rest = (part - high.astype(F32)).astype(BF16)
        row_sum = jnp.dot(
            jnp.concatenate([high, rest], axis=1), jnp.ones((2 * hd, hd), BF16), preferred_element_type=F32
        )
        merge(tile, picked, peak, row_sum, summed)
        if best is not None:
            peak_ref[...] = jnp.broadcast_to(jnp.max(best, axis=1, keepdims=True), peak_ref.shape)

    def start(tile, n_chunks, picked, valid):
        q = queries_of(picked)
        best = None
        for c in range(n_chunks):
            s = score(tile, c, n_chunks, q, valid)
            s_ref[:, c * chunk : (c + 1) * chunk] = s
            best = s if best is None else jnp.maximum(best, s)
        peak_ref[...] = jnp.broadcast_to(jnp.max(best, axis=1, keepdims=True), peak_ref.shape)

    def merge(tile, picked, peak, row_sum, summed):
        span = heads * SUB
        for i, block in enumerate(picked):
            src = pl.multiple_of(jnp.where(block == count, 0, block) * SUB, SUB)
            low = lohi_ref[pl.ds(src, SUB), :hd]
            high = lohi_ref[pl.ds(src, SUB), hd:]
            tile_f = tile.astype(F32)
            seen = jnp.where((low <= tile_f) & (tile_f < high), 1.0, 0.0)
            seen = jnp.concatenate([seen] * heads, axis=0)
            part_slice = slice(i * span, (i + 1) * span)
            mine = jnp.where(seen > 0.0, peak[part_slice], NEG)
            old = top[block]
            new = jnp.maximum(old, mine)
            keep = jnp.exp2((old - new) * factor)
            take = jnp.where(seen > 0.0, jnp.exp2((mine - new) * factor), 0.0)
            top[block] = new
            low_sum[block] = low_sum[block] * keep + row_sum[part_slice] * take
            acc[block] = acc[block] * keep + summed[part_slice] * take

    def one_tile(tile, carry):
        found = 0
        for block in range(count):
            blocks_of[found] = block
            found = found + flag_ref[block, tile]
        for i in range(2 * group):
            blocks_of[found + i] = count
        trips = (found + group - 1) // group
        valid = tokens_ref[tile]
        base = least // chunk
        extra = (valid - least + chunk - 1) // chunk

        def picked(i):
            return [blocks_of[i * group + j] for j in range(group)]

        for more in range((tile_len - least) // chunk + 1):

            @pl.when((extra == more) & (trips > 0))
            def _(more=more):
                start(tile, base + more, picked(0), valid)

                def pair(i, c):
                    step(tile, base + more, picked(i), picked(i + 1), valid)
                    return c

                lax.fori_loop(0, trips - 1, pair, 0)
                step(tile, base + more, picked(trips - 1), None, valid)

        return carry

    lax.fori_loop(0, tiles, one_tile, 0)

    def close(block, carry):
        src = block * SUB
        low = lohi_ref[pl.ds(src, SUB), :hd]
        high = lohi_ref[pl.ds(src, SUB), hd:]
        unseen = jnp.where(high <= low, 1.0, 0.0)
        unseen = jnp.concatenate([unseen] * heads, axis=0)
        done = (acc[block] / (low_sum[block] + unseen)).astype(BF16)
        for h in range(heads):
            sorted_out[pl.ds(src, SUB), h * hd : (h + 1) * hd] = done[h * SUB : (h + 1) * SUB]
        return carry

    for block in range(count):
        close(block, 0)
    out_ref[...] = jnp.dot(pt_ref[...], sorted_out[...], preferred_element_type=F32).astype(BF16)


def run_attend(tile_tokens, flags, kv, qs, pt, lohi, head_dim):
    text_rows, cols = qs.shape
    tile_len = kv.shape[0] // tile_tokens.shape[0]
    span = (cols // head_dim) * SUB
    blocks = text_rows // SUB
    smem = pl.BlockSpec(memory_space=pltpu.SMEM)
    vmem = pl.BlockSpec(memory_space=pltpu.VMEM)
    return pl.pallas_call(
        functools.partial(attend, head_dim ** (-0.5), tile_len, tile_len // 2),
        out_shape=jax.ShapeDtypeStruct((text_rows, cols), BF16),
        in_specs=[smem, smem, vmem, vmem, vmem, vmem],
        out_specs=vmem,
        scratch_shapes=[
            pltpu.VMEM((blocks + 1, span, head_dim), F32),
            pltpu.VMEM((blocks + 1, span, head_dim), F32),
            pltpu.VMEM((blocks + 1, span, head_dim), F32),
            pltpu.VMEM((text_rows, cols), BF16),
            pltpu.VMEM((4 * span, tile_len), F32),
            pltpu.VMEM((4 * span, head_dim), F32),
            pltpu.SMEM((blocks + 8,), jnp.int32),
        ],
        compiler_params=pltpu.CompilerParams(vmem_limit_bytes=40 << 20),
        name="attend",
    )(tile_tokens, flags, kv, qs, pt, lohi)


def shards(vision_states, kv_weight, key_gain, queries, tile_tokens, text_tiles):
    head_dim = key_gain.shape[0]
    rows = vision_states.shape[0]
    heads = lax.axis_size("tensor")
    nz = lax.axis_size("seq") // 2
    pieces = lax.axis_size("segment") * lax.axis_size("seq")
    depth = vision_states.shape[1]
    text_rows = queries.shape[0]
    q = queries.reshape(text_rows, queries.shape[2])
    vmem = pl.BlockSpec(memory_space=pltpu.VMEM)
    hbm = pl.BlockSpec(memory_space=pltpu.HBM)
    dma = pltpu.SemaphoreType.DMA
    kv, qs, pt, lohi, flags = pl.pallas_call(
        functools.partial(project_gather, nz),
        out_shape=(
            jax.ShapeDtypeStruct((pieces, rows, 2 * head_dim), BF16),
            jax.ShapeDtypeStruct(q.shape, BF16),
            jax.ShapeDtypeStruct((text_rows, text_rows), BF16),
            jax.ShapeDtypeStruct((text_rows, 2 * head_dim), F32),
            jax.ShapeDtypeStruct((text_rows // SUB, 128), jnp.int32),
        ),
        in_specs=[hbm] * 5,
        out_specs=(vmem,) * 5,
        scratch_shapes=[
            pltpu.VMEM((rows, depth), BF16),
            pltpu.VMEM((heads, depth, 2 * head_dim), BF16),
            pltpu.VMEM((1, head_dim), F32),
            pltpu.VMEM(q.shape, BF16),
            pltpu.VMEM((2, text_rows), jnp.int32),
            pltpu.VMEM((heads - 1, rows, head_dim), F32),
            pltpu.VMEM((heads - 1, rows, head_dim), F32),
            pltpu.VMEM((heads - 1, rows, head_dim), VALUE_PART),
            pltpu.VMEM((heads - 1, rows, head_dim), VALUE_PART),
            pltpu.VMEM((rows, 2 * head_dim), F32),
            dma((4,)), dma((heads,)), dma((2,)), dma((2,)),
            dma((2, nz // 2)), dma((2, nz // 2)), dma((2, nz // 2 + 1)), dma, dma, dma,
        ],
        compiler_params=pltpu.CompilerParams(
            collective_id=0, has_side_effects=True, vmem_limit_bytes=40 << 20
        ),
        name="project_gather",
    )(*(pltpu.with_memory_space_constraint(a, pltpu.HBM) for a in (vision_states, kv_weight, key_gain.reshape(1, head_dim), q, text_tiles.T)))
    kv = kv.reshape(pieces * rows, 2 * head_dim)
    out = run_attend(tile_tokens, flags, kv, qs, pt, lohi, head_dim)
    return out.reshape(queries.shape)


def solution(mesh):
    placed = (
        P(("segment", "seq"), "tensor"),
        P("tensor", None),
        P(),
        P("seq", "tensor", "segment"),
        P(),
        P("seq", None),
    )
    return jax.shard_map(
        shards, mesh=mesh, in_specs=placed, out_specs=P("seq", "tensor", "segment"), check_vma=False
    )
```

time: 86.1 us -> 60.5 us (0.70)
  Pallas kernels: 80.4 us -> 60.4 us
  local copies, waits for them, and re-layouts: 5.44 us -> 0.01 us
    pallas_call x1, Pallas kernels: 60.2 us -> 47.2 us  [shards(): pl.pallas_call(functools.partial(project_gather, nz), out_shape=(jax.Shap...]
    pallas_call x1, Pallas kernels: 20.1 us -> 13.2 us  [run_attend(): pl.pallas_call(functools.partial(attend, head_dim ** (-0.5), tile_len, ti...]
    unnamed x12 -> x2, local copies, waits for them, and re-layouts: 5.44 us -> 0.01 us
where the time goes in v2:
time: 60.5 us; the launch traced here: 60.4 us
  Pallas kernels  60.4 us (100%)
    pallas_call x1, Pallas kernels, shards(): pl.pallas_call(functools.partial(project_gather, nz), out_shape=(jax.Shap...  47.2 us
    pallas_call x1, Pallas kernels, run_attend(): pl.pallas_call(functools.partial(attend, head_dim ** (-0.5), tile_len, ti...  13.2 us

profile of v2, /device:TPU:1, one launch (start us, length us, event | category | flops | bytes accessed | tf_op | source)
XLA Modules:
  0.0 60.4 jit_solution(18192412260089396992)
XLA Ops:
  0.0 0.0 copy-start
  0.0 47.2 %project_gather.1 = (bf16[64,96,256]{2,1,0:T(8,128)(2,1)S(1)}, bf16[512,512]{1,0:T(8,128)(2,1)S(1)}, bf16[512,512]{1,0:T(8,128)(2,1)S(1)}, f32[512,256]{1,0:T(8,128)S(1)}, s32[32,128]{1,0:T(8,128)S(1)}) custom-call(bf16[96,960]{1,0:T(8,128)(2,1)} %vis_hbm.1, bf16[960,2048]{1,0:T(8,128)(2,1)} %w_hbm.1, f32[1,128]{1,0:T(1,128)} %bitcast.8, ...), custom_call_target="tpu_custom_call" | custom-call | tf_op jit(solution)/shard_map/project_gather/pallas_call | solution.py:430
  47.2 0.0 copy-done
  47.2 13.2 %attend.1 = bf16[512,512]{1,0:T(8,128)(2,1)} custom-call(s32[4]{0:T(128)S(1)} %copy-done, s32[32,128]{1,0:T(8,128)S(1)} %get-tuple-element.10.flag_ref, bf16[6144,256]{1,0:T(8,128)(2,1)S(1)} %bitcast.5, bf16[512,512]{1,0:T(8,128)(2,1)S(1)} %get-tuple-element.12.qs_ref, bf16[512,512]{1,0:T(8,128)(2,1)S(1)} %get-tuple-element.13.pt_ref, ...), custom_call_target="tpu_custom_call" | custom-call | tf_op jit(solution)/shard_map/attend/pallas_call | solution.py:399
Async XLA Ops:
  0.0 47.2 %copy-start = (s32[4]{0:T(128)S(1)}, s32[4]{0:T(128)}, u32[]{:S(2)}) copy-start(s32[4]{0:T(128)} %tokens_ref.1) | copy-start | bytes 52
